TPU v7x, 256 devices: a whole 4x4x8 slice. The times are simulated.
256 devices in a mesh: blk: 32 (over x, z_lo, core), uly: 8 (over y, z_hi).
Axes of the slice: x: 4, y: 4, z: 8 (z_hi: 2, z_lo: 4; z = z_hi * 4 + z_lo), core: 2. Of those that a mesh axis runs over, the one named last changes fastest.
Arguments:
- video_tokens: bfloat16 [12288, 3072], P(('blk', 'uly')), may hold values from -6 to 6
- text_tokens: bfloat16 [256, 3072], P('uly'), may hold values from -6 to 6
- video_modulation: bfloat16 [3, 3072], replicated, may hold values from -4 to 4
- text_modulation: bfloat16 [3, 3072], replicated, may hold values from -4 to 4
- video_projection: bfloat16 [3072, 3, 2048], P(None, None, 'uly'), may hold values from -0.109375 to 0.109375
- text_projection: bfloat16 [3072, 3, 2048], P(None, None, 'uly'), may hold values from -0.109375 to 0.109375
- video_output: bfloat16 [2048, 3072], P('uly'), may hold values from -0.125 to 0.125
- text_output: bfloat16 [2048, 3072], P('uly'), may hold values from -0.125 to 0.125
- video_gains: float32 [2, 128], replicated, may hold values from 1 to 12
- text_gains: float32 [2, 128], replicated, may hold values from 1 to 12
Outputs:
- video_attention: bfloat16 [12288, 3072], P(('blk', 'uly'))
- text_attention: bfloat16 [256, 3072], P('uly')
All inputs are finite; a program needn't handle non-finite values.
Results may differ from a plain program's by a relative error of at most 0.025.
The roundings to bfloat16 on the way count: a program that leaves them out, or rounds other values in their place, can miss the bound.
Values may be sent and summed in bfloat16 or wider, within the bound.
A program may use at most 128 MiB of HBM per device.

v0:
```python
import jax
import jax.numpy as jnp
from jax import lax
from jax.sharding import Mesh
from jax.sharding import PartitionSpec as P

HD = 128
BLK = ("blk_0", "blk_1", "blk_2")
ULY = ("uly_0", "uly_1")
BLK_ULY = ("blk_0", "blk_1", "blk_2", "uly_0", "uly_1")
EPS_NORM = 1e-06


def collected_together(x, axis):
    leaves = jax.tree.leaves(x)
    turns = sorted(range(len(leaves)), key=lambda k: -leaves[k].size)
    width = (1, *leaves[turns[0]].shape)[-1]
    lines = [
        jnp.pad(leaves[k].reshape(-1), (0, -leaves[k].size % width)).reshape(-1, width)
        for k in turns
    ]
    both, at, found = (lax.all_gather(jnp.concatenate(lines), axis), 0, {})
    for k, line in zip(turns, lines):
        slab = both[:, at : at + len(line)].reshape(len(both), -1)
        found[k] = slab[:, : leaves[k].size].reshape(-1, *leaves[k].shape)
        at += len(line)
    numbers = iter(range(len(leaves)))
    return jax.tree.map(lambda _: found[next(numbers)], x)


def merged_by_axis(x, axes, combine):
    for axis in axes:
        pieces = collected_together(
            jax.tree.map(
                lambda part, kind: part.astype(kind),
                x,
                jax.tree.map(lambda a: jnp.bfloat16 if a.dtype == jnp.float32 else a.dtype, x),
            ),
            axis,
        )
        widened = [
            jax.tree.map(lambda part, own: part[k].astype(own.dtype), pieces, x)
            for k in range(lax.axis_size(axis))
        ]
        x = widened[0]
        for partner_block in widened[1:]:
            x = combine(x, partner_block)
    return x


def summed_rows(terms, axes):
    subtotal = terms.astype(jnp.bfloat16)
    for axis in axes:
        subtotal = lax.psum_scatter(subtotal, axis, scatter_dimension=0, tiled=True)
    return subtotal.astype(jnp.float32)


def split_up(x, dim, length):
    before, after = (x.shape[:dim], x.shape[dim + 1 :])
    return jnp.moveaxis(x.reshape(*before, length, -1, *after), dim, 0)


def summed_on_arrival(x, axis, dim):
    length = lax.axis_size(axis)
    tiles = lax.all_to_all(split_up(x, dim, length), axis, 0, 0, tiled=True)
    return jnp.sum(tiles.astype(jnp.float32), axis=0)


def modulate(rows, factors):
    floats = rows.astype(jnp.float32)
    centre = floats - jnp.mean(floats, axis=-1, keepdims=True)
    spread = jnp.mean(centre * centre, axis=-1, keepdims=True)
    normed = centre / jnp.sqrt(spread + EPS_NORM)
    wide = factors.astype(jnp.float32)
    return (normed * (1.0 + wide[1]) + wide[0]).astype(jnp.bfloat16)


def head_norm(vectors, channel_gain):
    inverse = lax.rsqrt(jnp.mean(vectors * vectors, axis=-1, keepdims=True) + EPS_NORM)
    return (vectors * inverse * channel_gain).astype(jnp.bfloat16)


def project_rows(modded, weights, gains):
    mixture = jnp.einsum("td,dch->tch", modded, weights, preferred_element_type=jnp.float32)
    row_count, col_count = (mixture.shape[0], mixture.shape[2])
    per_head = mixture.reshape(row_count, 3, col_count // HD, HD)
    query_rows = head_norm(per_head[:, 0], gains[0]).reshape(row_count, col_count)
    key_rows = head_norm(per_head[:, 1], gains[1]).reshape(row_count, col_count)
    value_rows = per_head[:, 2].astype(jnp.bfloat16).reshape(row_count, col_count)
    return jnp.stack([query_rows, key_rows, value_rows], axis=1)


def block_scores(query_rows, key_rows):
    heads_here = query_rows.shape[1] // HD
    return jnp.einsum(
        "qhd,khd->hqk",
        query_rows.reshape(-1, heads_here, HD),
        key_rows.reshape(-1, heads_here, HD),
        preferred_element_type=jnp.float32,
    ) * HD ** (-0.5)


def weighted(weights, value_rows):
    heads_here = weights.shape[0]
    return jnp.einsum(
        "hqk,khd->hqd",
        weights.astype(jnp.bfloat16),
        value_rows.reshape(-1, heads_here, HD),
        preferred_element_type=jnp.float32,
    )


def opening(query_rows, key_rows, value_rows):
    scores = block_scores(query_rows, key_rows)
    highest = jnp.max(scores, axis=-1)
    weights = jnp.exp(scores - highest[..., None])
    return (highest, jnp.sum(weights, axis=-1), weighted(weights, value_rows))


def absorb(softmax_state, query_rows, key_rows, value_rows):
    highest, totals, weighted_sums = softmax_state
    scores = block_scores(query_rows, key_rows)
    raised = jnp.maximum(highest, jnp.max(scores, axis=-1))
    shrink = jnp.exp(highest - raised)
    weights = jnp.exp(scores - raised[..., None])
    return (
        raised,
        totals * shrink + jnp.sum(weights, axis=-1),
        weighted_sums * shrink[..., None] + weighted(weights, value_rows),
    )


def combine_states(earlier_state, later_state):
    raised = jnp.maximum(earlier_state[0], later_state[0])
    left_scale = jnp.exp(earlier_state[0] - raised)
    right_scale = jnp.exp(later_state[0] - raised)
    totals = earlier_state[1] * left_scale + later_state[1] * right_scale
    weighted_sums = (
        earlier_state[2] * left_scale[..., None] + later_state[2] * right_scale[..., None]
    )
    return (raised, totals, weighted_sums)


def finalize(softmax_state):
    result = softmax_state[2] / softmax_state[1][..., None]
    return jnp.transpose(result, (1, 0, 2)).reshape(result.shape[1], -1).astype(jnp.bfloat16)


def joint_attention(softmax_state, query_rows, pairs):
    shard_rows = pairs.shape[0]
    piece_rows = lax.all_gather(pairs, BLK, axis=0, tiled=True)
    turn_count = piece_rows.shape[0] // shard_rows
    turn_rows = piece_rows.shape[0] // turn_count

    def one_turn(turn_index, inner_state):
        sliced = lax.dynamic_slice_in_dim(piece_rows, turn_index * turn_rows, turn_rows, 0)
        return absorb(inner_state, query_rows, sliced[:, 0], sliced[:, 1])

    return lax.fori_loop(0, turn_count, one_turn, softmax_state)


def local(
    video_tokens,
    text_tokens,
    video_modulation,
    text_modulation,
    video_projection,
    text_projection,
    video_output,
    text_output,
    video_gains,
    text_gains,
):
    video_proj = project_rows(
        lax.all_gather(modulate(video_tokens, video_modulation), ULY, axis=0, tiled=True),
        video_projection,
        video_gains,
    )
    text_proj = project_rows(
        lax.all_gather(modulate(text_tokens, text_modulation), ULY, axis=0, tiled=True),
        text_projection,
        text_gains,
    )
    video_pairs = video_proj[:, 1:]
    video_state = opening(video_proj[:, 0], text_proj[:, 1], text_proj[:, 2])
    video_heads = finalize(joint_attention(video_state, video_proj[:, 0], video_pairs))
    text_state = opening(text_proj[:, 0], video_proj[:, 1], video_proj[:, 2])
    text_state = merged_by_axis(text_state, BLK, combine_states)
    text_heads = finalize(absorb(text_state, text_proj[:, 0], text_proj[:, 1], text_proj[:, 2]))
    video_summed = summed_rows(
        jnp.dot(video_heads, video_output, preferred_element_type=jnp.float32), ULY
    )
    text_summed = summed_on_arrival(
        jnp.dot(text_heads, text_output, preferred_element_type=jnp.float32).astype(jnp.bfloat16),
        ULY,
        0,
    )
    video_attention = (video_summed * video_modulation[2].astype(jnp.float32)).astype(jnp.bfloat16)
    text_attention = (text_summed * text_modulation[2].astype(jnp.float32)).astype(jnp.bfloat16)
    return (video_attention, text_attention)


def solution(mesh):
    torus = Mesh(mesh.devices.reshape(4, 4, 2, 4, 2), ("blk_0", "blk_1", "blk_2", "uly_0", "uly_1"))
    placed = (
        P(BLK_ULY, None),
        P(ULY, None),
        P(),
        P(),
        P(None, None, ULY),
        P(None, None, ULY),
        P(ULY, None),
        P(ULY, None),
        P(),
        P(),
    )
    return jax.shard_map(
        local,
        mesh=torus,
        in_specs=placed,
        out_specs=(P(BLK_ULY, None), P(ULY, None)),
        check_vma=False,
    )
```

profile of v0, /device:TPU:32, one launch (start us, length us, event | category | flops | bytes accessed | tf_op | source)
XLA Modules:
  0.0 410.6 jit_solution(2178064178969076653)
XLA Ops:
  8.9 1.1 convert_reduce_fusion.1
  10.0 1.2 fusion.17
  11.2 1.9 fusion.20
  14.6 80.3 %all-gather.7.cloned.1.call-done = bf16[384,3072]{1,0:T(8,128)(2,1)} async-done(((bf16[48,3072]{1,0:T(8,128)(2,1)}), bf16[384,3072]{1,0:T(8,128)(2,1)}) %all-gather.7.cloned.1.call-update) | async-done | bytes 2359312 | tf_op jit(solution)/shard_map/all_gather | solution.py:175
  94.9 5.3 %fusion.5 = f32[384,3,256]{0,2,1:T(8,128)S(1)} fusion(bf16[3072,3,256]{2,0,1:T(8,128)(2,1)} %param.16, bf16[384,3072]{1,0:T(8,128)(2,1)} %all-gather.7.cloned.1.call-done), kind=kOutput, calls=%fused_computation.14 | convolution fusion | flops 1811939328 | bytes 8257536 | tf_op jit(solution)/shard_map/td,dch->tch/dot_general | solution.py:84
  103.9 59.1 %all-gather.9.cloned.1.call-done = bf16[256,3072]{1,0:T(8,128)(2,1)} async-done(((bf16[32,3072]{1,0:T(8,128)(2,1)}), bf16[256,3072]{1,0:T(8,128)(2,1)}) %all-gather.9.cloned.1.call-update) | async-done | bytes 1572880 | tf_op jit(solution)/shard_map/all_gather | solution.py:180
  162.9 5.6 %fusion.7 = f32[256,3,256]{0,2,1:T(8,128)} fusion(bf16[3072,3,256]{2,0,1:T(8,128)(2,1)} %param.17, bf16[256,3072]{1,0:T(8,128)(2,1)} %all-gather.9.cloned.1.call-done), kind=kOutput, calls=%fused_computation.16 | convolution fusion | flops 1207959552 | bytes 7077888 | tf_op jit(solution)/shard_map/td,dch->tch/dot_general | solution.py:84
  171.9 1.2 fusion.156
  175.3 14.7 %all-gather = bf16[2080,128]{1,0:T(8,128)(2,1)S(1)} all-gather(bf16[520,128]{1,0:T(8,128)(2,1)S(1)} %pad_maximum_fusion.1), channel_id=2, replica_groups=mesh['blk_0'=4,'blk_1'=4,'blk_2'=2,'uly_0'=4,'uly_1'=2] {'blk_0'}, dimensions={0}, use_global_device_ids=true | all-gather | bytes 665600 | tf_op jit(solution)/shard_map/all_gather | solution.py:22
  191.7 52.5 %all-gather.11.cloned.1.call-done = bf16[12288,2,256]{0,2,1:T(8,128)(2,1)} async-done(((bf16[384,2,256]{0,2,1:T(8,128)(2,1)}), bf16[12288,2,256]{0,2,1:T(8,128)(2,1)}) %all-gather.11.cloned.1.call-update) | async-done | bytes 12582928 | tf_op jit(solution)/shard_map/all_gather | solution.py:151
  244.2 71.0 %while.17 = (s32[]{:T(128)}, f32[2,384]{1,0:T(2,128)S(1)}, f32[2,384]{1,0:T(2,128)S(1)}, f32[2,384,128]{2,1,0:T(8,128)S(1)}, bf16[12288,2,256]{0,2,1:T(8,128)(2,...) while((s32[]{:T(128)}, f32[2,384]{1,0:T(2,128)S(1)}, ...), condition=%wide.region_12.13_spmd, body=%wide.region_9.12_spmd.sunk | while | flops 152962560 | bytes 5750959 | solution.py:159
  246.4 1.1 constant_dynamic-slice_fusion.3
  248.7 1.1 constant_dynamic-slice_fusion.3
  250.9 1.1 constant_dynamic-slice_fusion.3
  253.1 1.1 constant_dynamic-slice_fusion.3
  255.3 1.1 constant_dynamic-slice_fusion.3
  315.5 2.2 convolution_convert_fusion
  317.7 15.7 %all-gather.1 = bf16[2080,128]{1,0:T(8,128)(2,1)S(1)} all-gather(bf16[520,128]{1,0:T(8,128)(2,1)S(1)} %pad_maximum_fusion.2), channel_id=3, replica_groups=mesh['blk_0'=4,'blk_1'=4,'blk_2'=2,'uly_0'=4,'uly_1'=2] {'blk_1'}, dimensions={0}, use_global_device_ids=true | all-gather | bytes 665600 | tf_op jit(solution)/shard_map/all_gather | solution.py:22
  334.0 2.0 all-gather.2
  337.8 1.8 convolution_convert_fusion.1
  339.5 6.8 %all-to-all-start = ((bf16[8,32,3072]{2,1,0:T(8,128)(2,1)}), bf16[8,32,3072]{2,1,0:T(8,128)(2,1)S(1)}, u32[]{:S(2)}, u32[]{:S(2)}) async-start(bf16[8,32,3072]{2,1,0:T(8,128)(2,1)} %bitcast.68), calls=%async_computation.2 | async-start | bytes 3145728 | tf_op jit(solution)/shard_map/all_to_all | solution.py:65
  346.4 4.9 %reduce-scatter.3.cloned.1.call-done = bf16[96,3072]{1,0:T(8,128)(2,1)} async-done(((bf16[384,3072]{1,0:T(8,128)(2,1)}), bf16[96,3072]{1,0:T(8,128)(2,1)}) %reduce-scatter.3.cloned.1.call-update) | async-done | bytes 589840 | tf_op jit(solution)/shard_map/reduce_scatter | solution.py:54
  351.4 50.1 %all-to-all-done = bf16[8,32,3072]{2,1,0:T(8,128)(2,1)S(1)} async-done(((bf16[8,32,3072]{2,1,0:T(8,128)(2,1)}), bf16[8,32,3072]{2,1,0:T(8,128)(2,1)S(1)}, u32[]{:S(2)}, u32[]{:S(2)}) %all-to-all-start) | async-done | bytes 1572896 | tf_op jit(solution)/shard_map/all_to_all | solution.py:65
  402.4 1.7 multiply_convert_fusion
  (327 shorter events, 81.3 us)
Async XLA Ops:
  7.2 308.3 %copy-start = (bf16[256,3072]{1,0:T(8,128)(2,1)S(1)}, bf16[256,3072]{1,0:T(8,128)(2,1)}, u32[]{:S(2)}) copy-start(bf16[256,3072]{1,0:T(8,128)(2,1)} %param.18) | copy-start | bytes 4718596
  7.2 6.0 %copy-start.9 = (bf16[3,3072]{1,0:T(4,128)(2,1)S(1)}, bf16[3,3072]{1,0:T(4,128)(2,1)}, u32[]{:S(2)}) copy-start(bf16[3,3072]{1,0:T(4,128)(2,1)} %param.15) | copy-start | bytes 55300
  7.2 6.0 %copy-start.3 = (bf16[32,3072]{1,0:T(8,128)(2,1)S(1)}, bf16[32,3072]{1,0:T(8,128)(2,1)}, u32[]{:S(2)}) copy-start(bf16[32,3072]{1,0:T(8,128)(2,1)} %param.13) | copy-start | bytes 589828
  7.2 7.4 %copy-start.10 = (f32[2,128]{1,0:T(2,128)S(1)}, f32[2,128]{1,0:T(2,128)}, u32[]{:S(2)}) copy-start(f32[2,128]{1,0:T(2,128)} %param.21) | copy-start | bytes 3076
  7.2 7.4 %copy-start.11 = (f32[2,128]{1,0:T(2,128)S(1)}, f32[2,128]{1,0:T(2,128)}, u32[]{:S(2)}) copy-start(f32[2,128]{1,0:T(2,128)} %param.20) | copy-start | bytes 3076
  7.2 87.7 %all-gather.7.cloned.1.call-start = ((), (), s32[]{:S(2)}) async-start(), calls=%async_computation.3 | async-start | bytes 2654208 | tf_op jit(solution)/shard_map/all_gather | solution.py:175
  13.1 149.8 %all-gather.9.cloned.1.call-start = ((), (), s32[]{:S(2)}) async-start(), calls=%async_computation.4 | async-start | bytes 1769472 | tf_op jit(solution)/shard_map/all_gather | solution.py:180
  14.5 229.7 %all-gather.11.cloned.1.call-start = ((), (), s32[]{:S(2)}) async-start(), calls=%async_computation.5 | async-start | bytes 12976128 | tf_op jit(solution)/shard_map/all_gather | solution.py:151
  102.1 0.9 copy-start.6
  103.8 247.5 %reduce-scatter.3.cloned.1.call-start = ((), (), s32[]{:S(2)}) async-start(), calls=%async_computation.6 | async-start | bytes 2949120 | tf_op jit(solution)/shard_map/reduce_scatter | solution.py:54
  171.3 1.8 copy-start.5
  174.9 15.6 %copy-start.1 = (f32[384,1,2,128]{3,0,2,1:T(8,128)S(1)}, f32[384,1,2,128]{3,0,2,1:T(8,128)}, u32[]{:S(2)}) copy-start(f32[384,1,2,128]{3,0,2,1:T(8,128)} %copy.54) | copy-start | bytes 1179652
  190.5 0.9 copy-start.7
  317.7 18.6 %copy-start.2 = (f32[2,256,256]{1,2,0:T(8,128)S(1)}, f32[2,256,256]{1,2,0:T(8,128)}, u32[]{:S(2)}) copy-start(f32[2,256,256]{1,2,0:T(8,128)} %get-tuple-element.171) | copy-start | bytes 1572868
  336.3 1.4 copy-start.4
  339.5 6.9 %copy-start.8 = (bf16[3,3072]{1,0:T(4,128)(2,1)S(1)}, bf16[3,3072]{1,0:T(4,128)(2,1)}, u32[]{:S(2)}) copy-start(bf16[3,3072]{1,0:T(4,128)(2,1)} %param.14) | copy-start | bytes 55300
  339.5 61.9 %all-to-all-start = ((bf16[8,32,3072]{2,1,0:T(8,128)(2,1)}), bf16[8,32,3072]{2,1,0:T(8,128)(2,1)S(1)}, u32[]{:S(2)}, u32[]{:S(2)}) async-start(bf16[8,32,3072]{2,1,0:T(8,128)(2,1)} %bitcast.68), calls=%async_computation.2 | async-start | bytes 3145728 | tf_op jit(solution)/shard_map/all_to_all | solution.py:65
  346.3 56.1 %reduce-scatter.5.cloned.1.call-start = ((), (), s32[]{:S(2)}) async-start(), calls=%async_computation.7 | async-start | bytes 884736 | tf_op jit(solution)/shard_map/reduce_scatter | solution.py:54
Sparse Core Ops, SparseCore 0:
  13.2 81.6 all-gather.6
  98.1 64.7 all-gather.8
  164.7 79.4 all-gather.10
  317.8 33.4 reduce-scatter.2
  353.7 44.8 reduce-scatter.4
where the time goes:
time: 412 us; the launch traced here: 411 us
  waiting for transfers between devices  247 us (60%)
  matrix products  46.4 us (11%)
  local copies, waits for them, and re-layouts  43.2 us (10%)
  blocking collectives  32.4 us (8%)
  other arithmetic  18.7 us (5%)
  between operations  14.3 us (3%)
  starting transfers between devices  7 us (2%)
    all_gather x1, waiting for transfers between devices, local(): lax.all_gather(modulate(video_tokens, video_modulation), ULY, axis=0, til...  80.3 us
    all_gather x1, waiting for transfers between devices, local(): lax.all_gather(modulate(text_tokens, text_modulation), ULY, axis=0, tiled...  59.1 us
    all_gather x1, waiting for transfers between devices, joint_attention(): piece_rows = lax.all_gather(pairs, BLK, axis=0, tiled=True)  52.5 us
    all_to_all x1, waiting for transfers between devices, summed_on_arrival(): tiles = lax.all_to_all(split_up(x, dim, length), axis, 0, 0, tiled=True)  50.1 us
    slice x32, local copies, waits for them, and re-layouts, one_turn(): return absorb(inner_state, query_rows, sliced[:, 0], sliced[:, 1])  34.2 us
    all_gather x3, blocking collectives, collected_together(): both, at, found = (lax.all_gather(jnp.concatenate(lines), axis), 0, {})  32.4 us
    dot_general x35, matrix products, weighted(): jnp.einsum('hqk,khd->hqd', weights.astype(jnp.bfloat16), value_rows.resha...  17.2 us
    dot_general x35, matrix products, block_scores(): jnp.einsum('qhd,khd->hqk', query_rows.reshape(-1, heads_here, HD), key_ro...  14.2 us
  transfers between devices with their start and end apart: 6, of which 5 were waited for; matrix products, arithmetic and copies ran while one was open for 7% of the time, Pallas kernels for 0%

commit v1 on v0

--- a/solution.py
+++ b/solution.py
@@ -148,7 +148,13 @@
 
 def joint_attention(softmax_state, query_rows, pairs):
     shard_rows = pairs.shape[0]
-    piece_rows = lax.all_gather(pairs, BLK, axis=0, tiled=True)
+    _launch_words = lambda slab_in: jnp.concatenate(
+        jax.lax.all_to_all(
+            jnp.stack([slab_in for _ in range(jax.lax.psum(1, BLK))], axis=0), BLK, 0, 0
+        ),
+        axis=0,
+    )
+    piece_rows = _launch_words(pairs)
     turn_count = piece_rows.shape[0] // shard_rows
     turn_rows = piece_rows.shape[0] // turn_count
 

time: 412 us -> 633 us (1.54)
  waiting for transfers between devices: 247 us -> 389 us
  matrix products: 46.4 us -> 76.7 us
  local copies, waits for them, and re-layouts: 43.2 us -> 73.2 us
  blocking collectives: 32.4 us -> 42.2 us
    all_to_all x0 -> x1, waiting for transfers between devices: none -> 161 us  [joint_attention(): jax.lax.all_to_all(jnp.stack([slab_in for _ in range(jax.lax.psum(1, BLK)...]
    all_gather x1 -> x0, waiting for transfers between devices: 52.5 us -> none  [joint_attention(): piece_rows = lax.all_gather(pairs, BLK, axis=0, tiled=True)]
    all_gather x1, waiting for transfers between devices: 59.1 us -> 92.3 us  [local(): lax.all_gather(modulate(text_tokens, text_modulation), ULY, axis=0, tiled...]
    dot_general x35, matrix products: 14.2 us -> 45.4 us  [block_scores(): jnp.einsum('qhd,khd->hqk', query_rows.reshape(-1, heads_here, HD), key_ro...]
    all_to_all x0 -> x1, local copies, waits for them, and re-layouts: none -> 16.6 us  [joint_attention(): jax.lax.all_to_all(jnp.stack([slab_in for _ in range(jax.lax.psum(1, BLK)...]
    while x32 -> x96, local copies, waits for them, and re-layouts: 0.08 us -> 10.4 us
    all_gather x3, blocking collectives: 32.4 us -> 42.2 us  [collected_together(): both, at, found = (lax.all_gather(jnp.concatenate(lines), axis), 0, {})]
    another operation x0 -> x1, local copies, waits for them, and re-layouts: none -> 6.6 us  [joint_attention(): jnp.stack([slab_in for _ in range(jax.lax.psum(1, BLK))], axis=0)]
  transfers between devices with their start and end apart: 6 -> 6, of which waited for: 5 -> 5; matrix products, arithmetic and copies ran while one was open for 7% -> 3% of each run, Pallas kernels for 0% -> 0%
where the time goes in v1:
time: 633 us; the launch traced here: 628 us
  waiting for transfers between devices  389 us (61%)
  matrix products  76.7 us (12%)
  local copies, waits for them, and re-layouts  73.2 us (12%)
  blocking collectives  42.2 us (7%)
  other arithmetic  19.3 us (3%)
  between operations  14.3 us (2%)
  starting transfers between devices  11.4 us (2%)
    all_to_all x1, waiting for transfers between devices, joint_attention(): jax.lax.all_to_all(jnp.stack([slab_in for _ in range(jax.lax.psum(1, BLK)...  161 us
    all_gather x1, waiting for transfers between devices, local(): lax.all_gather(modulate(text_tokens, text_modulation), ULY, axis=0, tiled...  92.3 us
    all_gather x1, waiting for transfers between devices, local(): lax.all_gather(modulate(video_tokens, video_modulation), ULY, axis=0, til...  81.8 us
    all_to_all x1, waiting for transfers between devices, summed_on_arrival(): tiles = lax.all_to_all(split_up(x, dim, length), axis, 0, 0, tiled=True)  48 us
    dot_general x35, matrix products, block_scores(): jnp.einsum('qhd,khd->hqk', query_rows.reshape(-1, heads_here, HD), key_ro...  45.4 us
    all_gather x3, blocking collectives, collected_together(): both, at, found = (lax.all_gather(jnp.concatenate(lines), axis), 0, {})  42.2 us
    slice x32, local copies, waits for them, and re-layouts, one_turn(): return absorb(inner_state, query_rows, sliced[:, 0], sliced[:, 1])  33.7 us
    dot_general x35, matrix products, weighted(): jnp.einsum('hqk,khd->hqd', weights.astype(jnp.bfloat16), value_rows.resha...  17.3 us
  transfers between devices with their start and end apart: 6, of which 5 were waited for; matrix products, arithmetic and copies ran while one was open for 3% of the time, Pallas kernels for 0%

profile of v1, /device:TPU:32, one launch (start us, length us, event | category | flops | bytes accessed | tf_op | source)
XLA Modules:
  0.0 628.3 jit_solution(13744087210492524389)
XLA Ops:
  11.2 1.9 fusion.20
  13.1 81.8 %all-gather.6.cloned.1.call-done = bf16[384,3072]{1,0:T(8,128)(2,1)} async-done(((bf16[48,3072]{1,0:T(8,128)(2,1)}), bf16[384,3072]{1,0:T(8,128)(2,1)}) %all-gather.6.cloned.1.call-update) | async-done | bytes 2359312 | tf_op jit(solution)/shard_map/all_gather | solution.py:181
  94.9 5.3 fusion.5
  101.8 6.6 %stack.5 = bf16[32,384,2,256]{1,3,2,0:T(8,128)(2,1)} broadcast(bf16[384,2,256]{0,2,1:T(8,128)(2,1)S(1)} %pad_maximum_fusion), dimensions={1,2,3} | broadcast | bytes 12976128 | tf_op jit(solution)/shard_map/stack | solution.py:153
  108.4 6.3 %all-to-all-start = ((bf16[32,384,2,256]{1,3,2,0:T(8,128)(2,1)}), bf16[32,384,2,256]{1,3,2,0:T(8,128)(2,1)}, u32[]{:S(2)}, u32[]{:S(2)}) async-start(bf16[32,384,2,256]{1,3,2,0:T(8,128)(2,1)} %stack.5), calls=%async_computation | async-start | bytes 25165824 | tf_op jit(solution)/shard_map/all_to_all | solution.py:152
  116.2 92.3 %all-gather.8.cloned.1.call-done = bf16[256,3072]{1,0:T(8,128)(2,1)} async-done(((bf16[32,3072]{1,0:T(8,128)(2,1)}), bf16[256,3072]{1,0:T(8,128)(2,1)}) %all-gather.8.cloned.1.call-update) | async-done | bytes 1572880 | tf_op jit(solution)/shard_map/all_gather | solution.py:186
  208.5 4.8 fusion.7
  214.1 1.8 fusion.153
  215.8 1.4 fusion.154
  219.9 23.1 %all-gather = bf16[2080,128]{1,0:T(8,128)(2,1)S(1)} all-gather(bf16[520,128]{1,0:T(8,128)(2,1)S(1)} %pad_maximum_fusion.1), channel_id=2, replica_groups=mesh['blk_0'=4,'blk_1'=4,'blk_2'=2,'uly_0'=4,'uly_1'=2] {'blk_0'}, dimensions={0}, use_global_device_ids=true | all-gather | bytes 665600 | tf_op jit(solution)/shard_map/all_gather | solution.py:22
  244.9 161.0 %all-to-all-done = bf16[32,384,2,256]{1,3,2,0:T(8,128)(2,1)} async-done(((bf16[32,384,2,256]{1,3,2,0:T(8,128)(2,1)}), bf16[32,384,2,256]{1,3,2,0:T(8,128)(2,1)}, u32[]{:S(2)}, u32[]{:S(2)}) %all-to-all-start) | async-done | bytes 12582944 | tf_op jit(solution)/shard_map/all_to_all | solution.py:152
  406.0 16.6 %copy.73 = bf16[32,384,2,256]{3,1,0,2:T(8,128)(2,1)} copy(bf16[32,384,2,256]{1,3,2,0:T(8,128)(2,1)} %all-to-all-done) | data formatting | bytes 25165824 | tf_op jit(solution)/shard_map/all_to_all | solution.py:152
  422.6 110.9 %while.17 = (s32[]{:T(128)}, f32[2,384]{1,0:T(2,128)S(1)}, f32[2,384]{1,0:T(2,128)S(1)}, f32[2,384,128]{2,1,0:T(8,128)S(1)}, bf16[12288,2,256]{2,0,1:T(8,128)(2,...) while((s32[]{:T(128)}, f32[2,384]{1,0:T(2,128)S(1)}, ...), condition=%wide.region_12.13_spmd, body=%wide.region_9.12_spmd.sunk | while | flops 152962560 | bytes 6537391 | solution.py:165
  423.8 1.3 fusion.175
  461.9 1.3 fusion.175
  517.4 1.3 fusion.175
  533.7 2.2 convolution_convert_fusion
  536.9 17.1 %all-gather.1 = bf16[2080,128]{1,0:T(8,128)(2,1)S(1)} all-gather(bf16[520,128]{1,0:T(8,128)(2,1)S(1)} %copy-done.5), channel_id=3, replica_groups=mesh['blk_0'=4,'blk_1'=4,'blk_2'=2,'uly_0'=4,'uly_1'=2] {'blk_1'}, dimensions={0}, use_global_device_ids=true | all-gather | bytes 665600 | tf_op jit(solution)/shard_map/all_gather | solution.py:22
  554.5 2.0 all-gather.2
  558.3 1.8 convolution_convert_fusion.1
  560.0 5.0 all-to-all-start.1
  565.1 6.0 reduce-scatter.3.cloned.1.call-done
  571.2 48.0 %all-to-all-done.1 = bf16[8,32,3072]{2,1,0:T(8,128)(2,1)S(1)} async-done(((bf16[8,32,3072]{2,1,0:T(8,128)(2,1)}), bf16[8,32,3072]{2,1,0:T(8,128)(2,1)S(1)}, u32[]{:S(2)}, u32[]{:S(2)}) %all-to-all-start.1) | async-done | bytes 1572896 | tf_op jit(solution)/shard_map/all_to_all | solution.py:65
  620.1 1.7 multiply_convert_fusion
  (394 shorter events, 121.5 us)
Async XLA Ops:
  7.2 526.6 %copy-start = (bf16[256,3072]{1,0:T(8,128)(2,1)S(1)}, bf16[256,3072]{1,0:T(8,128)(2,1)}, u32[]{:S(2)}) copy-start(bf16[256,3072]{1,0:T(8,128)(2,1)} %param.18) | copy-start | bytes 4718596
  7.2 5.9 copy-start.13
  7.2 5.9 copy-start.12
  7.2 87.7 %all-gather.6.cloned.1.call-start = ((), (), s32[]{:S(2)}) async-start(), calls=%async_computation.4 | async-start | bytes 2654208 | tf_op jit(solution)/shard_map/all_gather | solution.py:181
  100.2 1.0 copy-start.1
  108.4 6.4 %copy-start.8 = (bf16[3,3072]{1,0:T(4,128)(2,1)S(1)}, bf16[3,3072]{1,0:T(4,128)(2,1)}, u32[]{:S(2)}) copy-start(bf16[3,3072]{1,0:T(4,128)(2,1)} %param.15) | copy-start | bytes 55300
  108.4 6.4 %copy-start.3 = (bf16[32,3072]{1,0:T(8,128)(2,1)S(1)}, bf16[32,3072]{1,0:T(8,128)(2,1)}, u32[]{:S(2)}) copy-start(bf16[32,3072]{1,0:T(8,128)(2,1)} %param.13) | copy-start | bytes 589828
  108.4 297.5 %all-to-all-start = ((bf16[32,384,2,256]{1,3,2,0:T(8,128)(2,1)}), bf16[32,384,2,256]{1,3,2,0:T(8,128)(2,1)}, u32[]{:S(2)}, u32[]{:S(2)}) async-start(bf16[32,384,2,256]{1,3,2,0:T(8,128)(2,1)} %stack.5), calls=%async_computation | async-start | bytes 25165824 | tf_op jit(solution)/shard_map/all_to_all | solution.py:152
  114.8 93.7 %all-gather.8.cloned.1.call-start = ((), (), s32[]{:S(2)}) async-start(), calls=%async_computation.5 | async-start | bytes 1769472 | tf_op jit(solution)/shard_map/all_gather | solution.py:186
  116.1 455.0 %reduce-scatter.3.cloned.1.call-start = ((), (), s32[]{:S(2)}) async-start(), calls=%async_computation.6 | async-start | bytes 2949120 | tf_op jit(solution)/shard_map/reduce_scatter | solution.py:54
  213.7 30.9 %copy-start.6 = (bf16[256,1,2,128]{3,0,2,1:T(8,128)(2,1)}, bf16[256,1,2,128]{3,0,2,1:T(8,128)(2,1)S(1)}, u32[]{:S(2)}) copy-start(bf16[256,1,2,128]{3,0,2,1:T(8,128)(2,1)S(1)} %copy.98) | copy-start | bytes 393220
  536.0 0.9 copy-start.5
  536.9 20.0 %copy-start.11 = (f32[2,256]{1,0:T(2,128)S(1)}, f32[2,256]{1,0:T(2,128)}, u32[]{:S(2)}) copy-start(f32[2,256]{1,0:T(2,128)} %get-tuple-element.188) | copy-start | bytes 6148
  536.9 20.0 %copy-start.2 = (f32[2,256,256]{1,2,0:T(8,128)S(1)}, f32[2,256,256]{1,2,0:T(8,128)}, u32[]{:S(2)}) copy-start(f32[2,256,256]{1,2,0:T(8,128)} %get-tuple-element.189) | copy-start | bytes 1572868
  554.0 3.0 copy-start.7
  556.9 1.4 copy-start.4
  560.0 5.0 copy-start.9
  560.0 11.1 %copy-start.10 = (bf16[3,3072]{1,0:T(4,128)(2,1)S(1)}, bf16[3,3072]{1,0:T(4,128)(2,1)}, u32[]{:S(2)}) copy-start(bf16[3,3072]{1,0:T(4,128)(2,1)} %param.14) | copy-start | bytes 55300
  560.0 59.1 %all-to-all-start.1 = ((bf16[8,32,3072]{2,1,0:T(8,128)(2,1)}), bf16[8,32,3072]{2,1,0:T(8,128)(2,1)S(1)}, u32[]{:S(2)}, u32[]{:S(2)}) async-start(bf16[8,32,3072]{2,1,0:T(8,128)(2,1)} %bitcast.69), calls=%async_computation.3 | async-start | bytes 3145728 | tf_op jit(solution)/shard_map/all_to_all | solution.py:65
  565.0 55.1 %reduce-scatter.5.cloned.1.call-start = ((), (), s32[]{:S(2)}) async-start(), calls=%async_computation.7 | async-start | bytes 884736 | tf_op jit(solution)/shard_map/reduce_scatter | solution.py:54
Sparse Core Ops, SparseCore 0:
  13.2 81.6 all-gather.5
  118.7 89.7 all-gather.7
  536.1 34.9 reduce-scatter.2
  573.5 44.1 reduce-scatter.4
